TPU v7x, 256 devices: a whole 4x4x8 slice. The times are simulated.
256 devices in a mesh: dp: 16 (over z, core), expert: 16 (over y, x).
Axes of the slice: x: 4, y: 4, z: 8, core: 2. Of those that a mesh axis runs over, the one named last changes fastest.
Arguments:
- cotangent: bfloat16 [32768, 2048], P(('dp', 'expert')), may hold values from -6 to 6
- saved_gate_up: bfloat16 [32768, 8, 1536], P(('dp', 'expert')), may hold values from -6 to 6
- route_ids: int32 [32768, 8], P(('dp', 'expert')), may hold values from 0 to 31, all different within a row; in each aligned block of 128 rows (0 to 127, 128 to 255, ...) at most 64 rows name the same one
- route_weights: float32 [32768, 8], P(('dp', 'expert')), may hold values from 0.05 to 1
- w_down: bfloat16 [32, 768, 2048], P('expert', 'dp'), may hold values from -0.21875 to 0.21875
Outputs:
- grad_gate_up: bfloat16 [32768, 8, 1536], P(('dp', 'expert'))
- route_grad: float32 [32768, 8], P(('dp', 'expert'))
- grad_down: float32 [32, 768, 2048], P('expert', 'dp')
Inputs may be any that keep to these rules, and one draw needn't show every extreme that they name: `route_ids`: within the rows of one device (aligned blocks of 128 tokens), no expert is named by more than 64 routes, and in every draw some expert is named by exactly 64; the 8 experts of a token are distinct.
All inputs are finite; a program needn't handle non-finite values.
Results may differ from a plain program's by a relative error of at most 0.02.
Values may be sent and summed in bfloat16 or wider, within the bound.
A program may use at most 128 MiB of HBM per device.

v0:
```python
import jax
import jax.numpy as jnp
from jax import lax
from jax.sharding import PartitionSpec as P


def slot_counts(ids, experts):
    routes = ids.shape[-1]
    onehot = (ids[..., None] == jnp.arange(experts, dtype=jnp.int32)).astype(jnp.bfloat16)
    lower = (jnp.arange(routes)[:, None] > jnp.arange(routes)[None, :]).astype(jnp.bfloat16)
    before = jnp.einsum("rq,...qe->...re", lower, onehot, preferred_element_type=jnp.float32)
    return jnp.sum(before * onehot.astype(jnp.float32), axis=-1).astype(jnp.int32)


def local(cotangent, saved_gate_up, route_ids, route_weights, w_down):
    tokens, top = route_ids.shape
    width = cotangent.shape[1]
    hidden_units = saved_gate_up.shape[2] // 2
    owners = lax.axis_size("expert")
    replicas = lax.axis_size("dp")
    me = lax.axis_index("expert")
    local_experts = w_down.shape[0]
    experts = local_experts * owners
    capacity = min(tokens, 2 * tokens * top // experts)
    routes = tokens * top
    cot_group = lax.all_gather(cotangent, "expert", axis=0, tiled=True)
    ids_group = lax.all_gather(route_ids.reshape(1, routes), "expert", axis=0, tiled=True)
    full_down = lax.all_gather(w_down, "dp", axis=1, tiled=True)
    gate = saved_gate_up[:, :, :hidden_units].astype(jnp.float32)
    up = saved_gate_up[:, :, hidden_units:].astype(jnp.float32)
    sig = jax.nn.sigmoid(gate)
    act = gate * sig
    hidden = (act * up).astype(jnp.bfloat16)
    weights = route_weights[:, :, None]
    scaled = (weights * hidden.astype(jnp.float32)).astype(jnp.bfloat16)
    flat_ids = route_ids.reshape(routes)
    slot = slot_counts(flat_ids, experts)
    position = flat_ids * capacity + slot
    slot_ids = jnp.arange(experts * capacity, dtype=jnp.int32)
    match = position[None, :] == slot_ids[:, None]
    route_of_slot = jnp.sum(
        jnp.where(match, jnp.arange(routes, dtype=jnp.int32)[None, :], 0), axis=1
    )
    filled = jnp.any(match, axis=1)
    h_rows = jnp.where(
        filled[:, None],
        scaled.reshape(routes, hidden_units)[route_of_slot],
        jnp.zeros((), jnp.bfloat16),
    )
    h_send = h_rows.reshape(owners, local_experts, capacity, hidden_units)
    slot_all = slot_counts(ids_group, experts)
    mine = me * local_experts + jnp.arange(local_experts, dtype=jnp.int32)
    pos_all = ids_group * capacity + slot_all
    want = (mine[:, None] * capacity + jnp.arange(capacity, dtype=jnp.int32)[None, :]).reshape(-1)
    hit = pos_all[:, None, :] == want[None, :, None]
    token_of = jnp.sum(
        jnp.where(hit, (jnp.arange(routes, dtype=jnp.int32) // top)[None, None, :], 0), axis=2
    )
    rows = (jnp.arange(owners, dtype=jnp.int32)[:, None] * tokens + token_of).reshape(
        owners, local_experts, capacity
    )
    rows = jnp.transpose(rows, (1, 0, 2)).reshape(local_experts, owners * capacity)
    dy_recv = cot_group[rows]
    h_recv = lax.all_to_all(h_send, "expert", split_axis=0, concat_axis=2, tiled=True)[0]
    grads = jnp.einsum(
        "jsd,jfd->jsf", dy_recv, full_down, preferred_element_type=jnp.float32
    ).astype(jnp.bfloat16)
    back = lax.all_to_all(
        grads.reshape(1, local_experts, owners * capacity, hidden_units),
        "expert",
        split_axis=2,
        concat_axis=0,
        tiled=True,
    )
    parts = []
    for j in range(local_experts):
        part = jnp.einsum(
            "sf,sd->fd", h_recv[j], dy_recv[j], preferred_element_type=jnp.float32
        ).astype(jnp.bfloat16)
        parts.append(
            lax.psum_scatter(part, "dp", scatter_dimension=0, tiled=True).astype(jnp.float32)
        )
    grad_down = jnp.stack(parts)
    returned_rows = back.reshape(experts * capacity, hidden_units)[position]
    qf = returned_rows.reshape(tokens, top, hidden_units).astype(jnp.float32)
    route_grad = jnp.sum(qf * hidden.astype(jnp.float32), -1)
    d_hidden = weights * qf
    d_gate = d_hidden * up * sig * (1.0 + gate * (1.0 - sig))
    d_up = d_hidden * act
    grad_gate_up = jnp.concatenate([d_gate, d_up], -1).astype(jnp.bfloat16)
    return (grad_gate_up, route_grad, grad_down)


def solution(mesh):
    return jax.shard_map(
        local,
        mesh=mesh,
        in_specs=(
            P(("dp", "expert"), None),
            P(("dp", "expert"), None, None),
            P(("dp", "expert"), None),
            P(("dp", "expert"), None),
            P("expert", "dp", None),
        ),
        out_specs=(
            P(("dp", "expert"), None, None),
            P(("dp", "expert"), None),
            P("expert", "dp", None),
        ),
        check_vma=False,
    )
```

profile of v0, /device:TPU:2, one launch (start us, length us, event | category | flops | bytes accessed | tf_op | source)
XLA Modules:
  0.0 409.4 jit_solution(11496074652841021074)
XLA Ops:
  7.2 0.0 all-gather.4.cloned.1.call-start
  7.2 0.7 all-gather.4.cloned.1.call-update
  7.9 0.0 all-gather.6.cloned.1.call-start
  7.9 0.7 all-gather.6.cloned.1.call-update
  8.7 0.8 copy.30
  9.4 0.1 reshape.205
  9.5 23.6 %all-gather = s32[16,1,1024]{2,1,0:T(1,128)S(1)} all-gather(s32[1,1,1024]{2,1,0:T(1,128)S(1)} %reshape.205), channel_id=1, replica_groups=mesh['dp'=16,'expert'=16] {'expert'}, dimensions={0}, use_global_device_ids=true | all-gather | bytes 69632 | tf_op jit(solution)/shard_map/all_gather | solution.py:27
  33.2 0.1 iota_add_fusion
  33.3 0.1 add.119
  33.4 1.4 fusion.27
  34.8 1.0 select_reduce_fusion.1
  35.8 0.1 reduce_sum.51
  35.9 0.1 add_bitcast_fusion
  36.0 0.1 reshape.171
  36.1 53.2 %all-gather.4.cloned.1.call-done = bf16[2048,2048]{1,0:T(8,128)(2,1)} async-done(((bf16[128,2048]{1,0:T(8,128)(2,1)}), bf16[2048,2048]{1,0:T(8,128)(2,1)}) %all-gather.4.cloned.1.call-update) | async-done | bytes 8388624 | tf_op jit(solution)/shard_map/all_gather | solution.py:26
  89.3 20.8 %gather_fusion = bf16[2048,2048]{1,0:T(8,128)(2,1)} fusion(bf16[2048,2048]{1,0:T(8,128)(2,1)} %all-gather.4.cloned.1.call-done, s32[2048]{0:T(1024)S(1)} %bitcast_clamp_fusion), kind=kCustom, calls=%fused_computation | custom fusion | bytes 16785408 | tf_op jit(solution)/shard_map/gather | solution.py:63
  110.1 26.9 %all-gather.6.cloned.1.call-done = bf16[2,768,2048]{2,1,0:T(8,128)(2,1)} async-done(((bf16[2,48,2048]{2,1,0:T(8,128)(2,1)}), bf16[2,768,2048]{2,1,0:T(8,128)(2,1)}) %all-gather.6.cloned.1.call-update) | async-done | bytes 6291472 | tf_op jit(solution)/shard_map/all_gather | solution.py:28
  136.9 11.0 %convert_bitcast_fusion = bf16[1,2,1024,768]{3,2,1,0:T(8,128)(2,1)S(1)} fusion(bf16[2,1024,2048]{2,1,0:T(8,128)(2,1)} %bitcast.55, bf16[2,768,2048]{2,1,0:T(8,128)(2,1)} %all-gather.6.cloned.1.call-done), kind=kOutput, calls=%fused_computation.38 | convolution fusion | flops 6444023808 | bytes 17825792 | tf_op jit(solution)/shard_map/jsd,jfd->jsf/dot_general | solution.py:65
  147.9 4.9 %copy.32 = bf16[1,2,1024,768]{3,1,0,2:T(2,128)(2,1)} copy(bf16[1,2,1024,768]{3,2,1,0:T(8,128)(2,1)S(1)} %convert_bitcast_fusion) | data formatting | bytes 6291456 | tf_op jit(solution)/shard_map/reshape | solution.py:69
  152.8 7.4 %all-to-all-start = ((bf16[1,2,1024,768]{3,1,0,2:T(2,128)(2,1)}), bf16[1,2,1024,768]{3,1,0,2:T(2,128)(2,1)S(1)}, u32[]{:S(2)}, u32[]{:S(2)}) async-start(bf16[1,2,1024,768]{3,1,0,2:T(2,128)(2,1)} %copy.32), calls=%async_computation | async-start | bytes 6291456 | tf_op jit(solution)/shard_map/all_to_all | solution.py:68
  160.2 0.0 reduce-scatter.5.cloned.1.call-start
  160.3 0.1 eq.60
  160.4 0.1 copy.29
  160.5 0.1 copy.34
  160.6 0.1 mul.102
  160.7 0.5 fusion.31
  161.3 1.0 fusion
  162.3 0.1 broadcast_in_dim.36
  162.4 0.9 select_reduce_fusion
  163.4 41.3 %all-to-all-done = bf16[1,2,1024,768]{3,1,0,2:T(2,128)(2,1)S(1)} async-done(((bf16[1,2,1024,768]{3,1,0,2:T(2,128)(2,1)}), bf16[1,2,1024,768]{3,1,0,2:T(2,128)(2,1)S(1)}, u32[]{:S(2)}, u32[]{:S(2)}) %all-to-all-start) | async-done | bytes 3145760 | tf_op jit(solution)/shard_map/all_to_all | solution.py:68
  204.7 1.7 copy-done.1
  206.3 2.5 copy.33
  208.9 5.2 %gather_fusion.1 = bf16[1024,768]{1,0:T(8,128)(2,1)} fusion(bf16[2048,768]{1,0:T(8,128)(2,1)S(1)} %bitcast.51, s32[1024]{0:T(1024)S(1)} %broadcast_clamp_fusion.1), kind=kCustom, calls=%fused_computation.1 | custom fusion | bytes 3149824 | tf_op jit(solution)/shard_map/gather | solution.py:84
  214.1 5.0 %fusion.29 = (bf16[1024,768]{1,0:T(8,128)(2,1)S(1)}, bf16[128,8,768]{2,1,0:T(8,128)(2,1)S(1)}, bf16[128,8,768]{2,1,0:T(8,128)(2,1)}, bf16[128,8,768]{2,1,0:T(8,128)(2,1)}) fusion(f32[128,8]{1,0:T(8,128)S(1)} %copy.29, bf16[128,8,1536]{2,1,0:T(8,128)(2,1)} %param.6, bf16[1024,768]{1,0:T(8,128)(2,1)} %gather_fusion.1), kind=kLoop, calls=%fused_computation.44 | loop fusion | flops 17301504 | bytes 11014144 | tf_op jit(solution)/shard_map/reshape | solution.py:47
  219.0 9.4 %gather_fusion.2 = bf16[2048,768]{1,0:T(8,128)(2,1)} fusion(bf16[1024,768]{1,0:T(8,128)(2,1)S(1)} %get-tuple-element.9, s32[2048]{0:T(1024)S(1)} %broadcast_clamp_fusion), kind=kCustom, calls=%fused_computation.2 | custom fusion | bytes 6299648 | tf_op jit(solution)/shard_map/gather | solution.py:47
  228.4 2.3 broadcast_select_fusion
  230.7 46.5 %all_to_all.30 = bf16[16,2,64,768]{3,2,1,0:T(8,128)(2,1)S(1)} all-to-all(bf16[16,2,64,768]{3,2,1,0:T(8,128)(2,1)S(1)} %broadcast_select_fusion), channel_id=1, replica_groups=mesh['dp'=16,'expert'=16] {'expert'}, dimensions={0} | all-to-all | bytes 6291456 | tf_op jit(solution)/shard_map/all_to_all | solution.py:64
  277.2 0.2 fusion.42
  277.5 4.9 %fusion.13 = bf16[768,2048]{1,0:T(8,128)(2,1)} fusion(bf16[1024,768]{1,0:T(8,128)(2,1)S(1)} %bitcast.59, bf16[2048,2048]{1,0:T(8,128)(2,1)S(1)} %bitcast.57), kind=kOutput, calls=%fused_computation.25 | convolution fusion | flops 3222798336 | bytes 8912896 | tf_op jit(solution)/shard_map/sf,sd->fd/dot_general | solution.py:77
  282.4 0.0 reduce-scatter.3.cloned.1.call-start
  282.5 7.0 %fusion.10 = bf16[768,2048]{1,0:T(8,128)(2,1)} fusion(bf16[1024,768]{1,0:T(8,128)(2,1)S(1)} %bitcast.58, bf16[2048,2048]{1,0:T(8,128)(2,1)} %gather_fusion), kind=kOutput, calls=%fused_computation.24 | convolution fusion | flops 3222798336 | bytes 8912896 | tf_op jit(solution)/shard_map/sf,sd->fd/dot_general | solution.py:77
  289.6 1.4 copy-done
  290.9 0.5 fusion.22
  291.4 0.7 copy.36
  292.1 3.8 pad_maximum_fusion
  295.9 43.3 %reduce-scatter.5.cloned.1.call-done = bf16[48,2048]{1,0:T(8,128)(2,1)} async-done(((bf16[768,2048]{1,0:T(8,128)(2,1)}), bf16[48,2048]{1,0:T(8,128)(2,1)}) %reduce-scatter.5.cloned.1.call-update) | async-done | bytes 196624 | tf_op jit(solution)/shard_map/reduce_scatter | solution.py:81
  339.2 61.7 %reduce-scatter.3.cloned.1.call-done = bf16[48,2048]{1,0:T(8,128)(2,1)} async-done(((bf16[768,2048]{1,0:T(8,128)(2,1)}), bf16[48,2048]{1,0:T(8,128)(2,1)}) %reduce-scatter.3.cloned.1.call-update) | async-done | bytes 196624 | tf_op jit(solution)/shard_map/reduce_scatter | solution.py:81
  400.9 2.0 maximum_convert_fusion
  (28 shorter events, 0.2 us)
Async XLA Ops:
  7.2 82.1 %all-gather.4.cloned.1.call-start = ((), (), s32[]{:S(2)}) async-start(), calls=%async_computation.4 | async-start | bytes 8912896 | tf_op jit(solution)/shard_map/all_gather | solution.py:26
  7.9 129.0 %all-gather.6.cloned.1.call-start = ((), (), s32[]{:S(2)}) async-start(), calls=%async_computation.5 | async-start | bytes 6684672 | tf_op jit(solution)/shard_map/all_gather | solution.py:28
  152.8 7.5 %copy-start.3 = (f32[128,8]{0,1:T(8,128)S(1)}, f32[128,8]{0,1:T(8,128)}, u32[]{:S(2)}) copy-start(f32[128,8]{0,1:T(8,128)} %param.8) | copy-start | bytes 12292
  152.8 7.7 %copy-start.2 = (s32[128,8]{0,1:T(8,128)S(1)}, s32[128,8]{0,1:T(8,128)}, u32[]{:S(2)}) copy-start(s32[128,8]{0,1:T(8,128)} %param.7) | copy-start | bytes 12292
  152.8 51.8 %all-to-all-start = ((bf16[1,2,1024,768]{3,1,0,2:T(2,128)(2,1)}), bf16[1,2,1024,768]{3,1,0,2:T(2,128)(2,1)S(1)}, u32[]{:S(2)}, u32[]{:S(2)}) async-start(bf16[1,2,1024,768]{3,1,0,2:T(2,128)(2,1)} %copy.32), calls=%async_computation | async-start | bytes 6291456 | tf_op jit(solution)/shard_map/all_to_all | solution.py:68
  160.2 179.0 %reduce-scatter.5.cloned.1.call-start = ((), (), s32[]{:S(2)}) async-start(), calls=%async_computation.7 | async-start | bytes 3342336 | tf_op jit(solution)/shard_map/reduce_scatter | solution.py:81
  204.7 1.7 copy-start.1
  228.4 49.1 %slice-start = ((s8[8388608]{0:T(1024)(128)(4,1)}), s8[4194304]{0:T(1024)(128)(4,1)S(1)}, s32[]{:S(2)}) async-start(s8[8388608]{0:T(1024)(128)(4,1)} %bitcast.56), calls=%async_computation.8 | async-start | bytes 8388608
  230.7 46.8 %slice-start.1 = ((s8[8388608]{0:T(1024)(128)(4,1)}), s8[4194304]{0:T(1024)(128)(4,1)S(1)}, s32[]{:S(2)}) async-start(s8[8388608]{0:T(1024)(128)(4,1)} %bitcast.56), calls=%async_computation.9 | async-start | bytes 8388608
  282.4 118.5 %reduce-scatter.3.cloned.1.call-start = ((), (), s32[]{:S(2)}) async-start(), calls=%async_computation.6 | async-start | bytes 3342336 | tf_op jit(solution)/shard_map/reduce_scatter | solution.py:81
  289.5 1.4 copy-start
Sparse Core Ops, SparseCore 0:
  10.4 78.7 all-gather.3
  91.1 45.7 all-gather.5
  282.6 56.6 reduce-scatter.4
  341.6 59.2 reduce-scatter.2
where the time goes:
time: 410 us; the launch traced here: 409 us
  waiting for transfers between devices  228 us (56%)
  blocking collectives  70.2 us (17%)
  local copies, waits for them, and re-layouts  48.4 us (12%)
  matrix products  24.9 us (6%)
  other arithmetic  16.6 us (4%)
  between operations  14 us (3%)
  starting transfers between devices  7.56 us (2%)
    reduce_scatter x2, waiting for transfers between devices, local(): lax.psum_scatter(part, 'dp', scatter_dimension=0, tiled=True)  105 us
    all_gather x1, waiting for transfers between devices, local(): cot_group = lax.all_gather(cotangent, 'expert', axis=0, tiled=True)  53.2 us
    all_to_all x1, blocking collectives, local(): lax.all_to_all(h_send, 'expert', split_axis=0, concat_axis=2, tiled=True)[0]  46.5 us
    all_to_all x1, waiting for transfers between devices, local(): lax.all_to_all(grads.reshape(1, local_experts, owners * capacity, hidden_...  41.3 us
    all_gather x1, waiting for transfers between devices, local(): full_down = lax.all_gather(w_down, 'dp', axis=1, tiled=True)  26.9 us
    all_gather x1, blocking collectives, local(): lax.all_gather(route_ids.reshape(1, routes), 'expert', axis=0, tiled=True)  23.6 us
    gather x1, local copies, waits for them, and re-layouts, local(): dy_recv = cot_group[rows]  20.8 us
    dot_general x2, matrix products, local(): jnp.einsum('sf,sd->fd', h_recv[j], dy_recv[j], preferred_element_type=jnp...  11.9 us
  transfers between devices with their start and end apart: 5, of which 5 were waited for; matrix products, arithmetic and copies ran while one was open for 10% of the time, Pallas kernels for 0%

commit v1 on v0

--- a/solution.py
+++ b/solution.py
@@ -23,7 +23,9 @@
     experts = local_experts * owners
     capacity = min(tokens, 2 * tokens * top // experts)
     routes = tokens * top
-    cot_group = lax.all_gather(cotangent, "expert", axis=0, tiled=True)
+    cot_group = jnp.concatenate(
+        lax.all_to_all(jnp.stack([cotangent] * lax.axis_size("expert")), "expert", 0, 0), axis=0
+    )
     ids_group = lax.all_gather(route_ids.reshape(1, routes), "expert", axis=0, tiled=True)
     full_down = lax.all_gather(w_down, "dp", axis=1, tiled=True)
     gate = saved_gate_up[:, :, :hidden_units].astype(jnp.float32)

time: 410 us -> 445 us (1.085)
  blocking collectives: 70.2 us -> 181 us
  waiting for transfers between devices: 228 us -> 142 us
  starting transfers between devices: 7.56 us -> 13.5 us
  local copies, waits for them, and re-layouts: 48.4 us -> 53.1 us
    all_gather x1, blocking collectives: 23.6 us -> 137 us  [local(): lax.all_gather(route_ids.reshape(1, routes), 'expert', axis=0, tiled=True)]
    all_gather x1 -> x0, waiting for transfers between devices: 53.2 us -> none  [local(): cot_group = lax.all_gather(cotangent, 'expert', axis=0, tiled=True)]
    all_gather x1, waiting for transfers between devices: 26.9 us -> 0.01 us  [local(): full_down = lax.all_gather(w_down, 'dp', axis=1, tiled=True)]
    all_to_all x1, waiting for transfers between devices: 41.3 us -> 31.4 us  [local(): lax.all_to_all(grads.reshape(1, local_experts, owners * capacity, hidden_...]
    all_to_all x0 -> x1, starting transfers between devices: none -> 7.61 us  [local(): lax.all_to_all(jnp.stack([cotangent] * lax.axis_size('expert')), 'expert'...]
    another operation x0 -> x1, local copies, waits for them, and re-layouts: none -> 5.33 us  [local(): jnp.stack([cotangent] * lax.axis_size('expert'))]
    reduce_scatter x2, waiting for transfers between devices: 105 us -> 110 us  [local(): lax.psum_scatter(part, 'dp', scatter_dimension=0, tiled=True)]
  transfers between devices with their start and end apart: 5 -> 5, of which waited for: 5 -> 3; matrix products, arithmetic and copies ran while one was open for 10% -> 10% of each run, Pallas kernels for 0% -> 0%
where the time goes in v1:
time: 445 us
  blocking collectives  181 us (41%)
  waiting for transfers between devices  142 us (32%)
  local copies, waits for them, and re-layouts  53.1 us (12%)
  matrix products  24.9 us (6%)
  other arithmetic  16.7 us (4%)
  between operations  14 us (3%)
  starting transfers between devices  13.5 us (3%)
    all_gather x1, blocking collectives, local(): lax.all_gather(route_ids.reshape(1, routes), 'expert', axis=0, tiled=True)  137 us
    reduce_scatter x2, waiting for transfers between devices, local(): lax.psum_scatter(part, 'dp', scatter_dimension=0, tiled=True)  110 us
    all_to_all x1, blocking collectives, local(): lax.all_to_all(h_send, 'expert', split_axis=0, concat_axis=2, tiled=True)[0]  44.4 us
    all_to_all x1, waiting for transfers between devices, local(): lax.all_to_all(grads.reshape(1, local_experts, owners * capacity, hidden_...  31.4 us
    gather x1, local copies, waits for them, and re-layouts, local(): dy_recv = cot_group[rows]  20.8 us
    dot_general x2, matrix products, local(): jnp.einsum('sf,sd->fd', h_recv[j], dy_recv[j], preferred_element_type=jnp...  12 us
    dot_general x1, matrix products, local(): jnp.einsum('jsd,jfd->jsf', dy_recv, full_down, preferred_element_type=jnp...  11 us
    gather x1, local copies, waits for them, and re-layouts, local(): scaled.reshape(routes, hidden_units)[route_of_slot]  9.4 us
  transfers between devices with their start and end apart: 5, of which 3 were waited for; matrix products, arithmetic and copies ran while one was open for 10% of the time, Pallas kernels for 0%

profile of v1, /device:TPU:2, one launch (start us, length us, event | category | flops | bytes accessed | tf_op | source)
XLA Modules:
  0.0 444.7 jit_solution(17293842754861907576)
XLA Ops:
  7.2 0.0 all-gather.3.cloned.1.call-start
  7.2 0.7 all-gather.3.cloned.1.call-update
  7.9 5.3 %stack.13 = bf16[16,128,2048]{2,1,0:T(8,128)(2,1)} broadcast(bf16[128,2048]{1,0:T(8,128)(2,1)} %param.5), dimensions={1,2} | broadcast | bytes 8912896 | tf_op jit(solution)/shard_map/stack | solution.py:27
  13.2 7.6 %all-to-all-start = ((bf16[16,128,2048]{2,1,0:T(8,128)(2,1)}), bf16[16,128,2048]{2,1,0:T(8,128)(2,1)}, u32[]{:S(2)}, u32[]{:S(2)}) async-start(bf16[16,128,2048]{2,1,0:T(8,128)(2,1)} %stack.13), calls=%async_computation | async-start | bytes 16777216 | tf_op jit(solution)/shard_map/all_to_all | solution.py:27
  20.8 0.1 copy.30
  20.9 0.1 reshape.211
  21.0 136.6 %all-gather = s32[16,1,1024]{2,1,0:T(1,128)S(1)} all-gather(s32[1,1,1024]{2,1,0:T(1,128)S(1)} %reshape.211), channel_id=1, replica_groups=mesh['dp'=16,'expert'=16] {'expert'}, dimensions={0}, use_global_device_ids=true | all-gather | bytes 69632 | tf_op jit(solution)/shard_map/all_gather | solution.py:29
  157.7 0.1 iota_add_fusion
  157.8 0.1 add.119
  157.9 1.4 fusion.27
  159.3 1.0 select_reduce_fusion.1
  160.3 0.1 reduce_sum.51
  160.3 0.1 add_bitcast_fusion
  160.4 0.1 reshape.177
  160.6 20.8 %gather_fusion = bf16[2048,2048]{1,0:T(8,128)(2,1)} fusion(bf16[2048,2048]{1,0:T(8,128)(2,1)} %bitcast, s32[2048]{0:T(1024)S(1)} %bitcast_clamp_fusion), kind=kCustom, calls=%fused_computation | custom fusion | bytes 16785408 | tf_op jit(solution)/shard_map/gather | solution.py:65
  181.4 11.0 %convert_bitcast_fusion = bf16[1,2,1024,768]{3,2,1,0:T(8,128)(2,1)S(1)} fusion(bf16[2,1024,2048]{2,1,0:T(8,128)(2,1)} %bitcast.56, bf16[2,768,2048]{2,1,0:T(8,128)(2,1)} %all-gather.3.cloned.1.call-done), kind=kOutput, calls=%fused_computation.38 | convolution fusion | flops 6444023808 | bytes 17825792 | tf_op jit(solution)/shard_map/jsd,jfd->jsf/dot_general | solution.py:67
  192.4 4.9 %copy.32 = bf16[1,2,1024,768]{3,1,0,2:T(2,128)(2,1)} copy(bf16[1,2,1024,768]{3,2,1,0:T(8,128)(2,1)S(1)} %convert_bitcast_fusion) | data formatting | bytes 6291456 | tf_op jit(solution)/shard_map/reshape | solution.py:71
  197.3 5.6 %all-to-all-start.1 = ((bf16[1,2,1024,768]{3,1,0,2:T(2,128)(2,1)}), bf16[1,2,1024,768]{3,1,0,2:T(2,128)(2,1)S(1)}, u32[]{:S(2)}, u32[]{:S(2)}) async-start(bf16[1,2,1024,768]{3,1,0,2:T(2,128)(2,1)} %copy.32), calls=%async_computation.1 | async-start | bytes 6291456 | tf_op jit(solution)/shard_map/all_to_all | solution.py:70
  202.8 0.2 reduce-scatter.5.cloned.1.call-start
  203.0 0.1 eq.60
  203.1 0.1 copy.29
  203.3 0.1 copy.34
  203.4 0.1 mul.102
  203.5 0.5 fusion.31
  204.0 1.0 fusion
  205.1 0.1 broadcast_in_dim.36
  205.2 0.9 select_reduce_fusion
  206.1 31.4 %all-to-all-done.1 = bf16[1,2,1024,768]{3,1,0,2:T(2,128)(2,1)S(1)} async-done(((bf16[1,2,1024,768]{3,1,0,2:T(2,128)(2,1)}), bf16[1,2,1024,768]{3,1,0,2:T(2,128)(2,1)S(1)}, u32[]{:S(2)}, u32[]{:S(2)}) %all-to-all-start.1) | async-done | bytes 3145760 | tf_op jit(solution)/shard_map/all_to_all | solution.py:70
  237.5 1.7 copy-done.1
  239.1 2.5 copy.33
  241.7 5.2 %gather_fusion.1 = bf16[1024,768]{1,0:T(8,128)(2,1)} fusion(bf16[2048,768]{1,0:T(8,128)(2,1)S(1)} %bitcast.52, s32[1024]{0:T(1024)S(1)} %broadcast_clamp_fusion.1), kind=kCustom, calls=%fused_computation.1 | custom fusion | bytes 3149824 | tf_op jit(solution)/shard_map/gather | solution.py:86
  246.9 5.0 %fusion.29 = (bf16[1024,768]{1,0:T(8,128)(2,1)S(1)}, bf16[128,8,768]{2,1,0:T(8,128)(2,1)S(1)}, bf16[128,8,768]{2,1,0:T(8,128)(2,1)}, bf16[128,8,768]{2,1,0:T(8,128)(2,1)}) fusion(f32[128,8]{1,0:T(8,128)S(1)} %copy.29, bf16[128,8,1536]{2,1,0:T(8,128)(2,1)} %param.6, bf16[1024,768]{1,0:T(8,128)(2,1)} %gather_fusion.1), kind=kLoop, calls=%fused_computation.44 | loop fusion | flops 17301504 | bytes 11014144 | tf_op jit(solution)/shard_map/reshape | solution.py:49
  251.9 9.4 %gather_fusion.2 = bf16[2048,768]{1,0:T(8,128)(2,1)} fusion(bf16[1024,768]{1,0:T(8,128)(2,1)S(1)} %get-tuple-element.9, s32[2048]{0:T(1024)S(1)} %broadcast_clamp_fusion), kind=kCustom, calls=%fused_computation.2 | custom fusion | bytes 6299648 | tf_op jit(solution)/shard_map/gather | solution.py:49
  261.3 2.3 broadcast_select_fusion
  263.5 44.4 %all_to_all.35 = bf16[16,2,64,768]{3,2,1,0:T(8,128)(2,1)S(1)} all-to-all(bf16[16,2,64,768]{3,2,1,0:T(8,128)(2,1)S(1)} %broadcast_select_fusion), channel_id=1, replica_groups=mesh['dp'=16,'expert'=16] {'expert'}, dimensions={0} | all-to-all | bytes 6291456 | tf_op jit(solution)/shard_map/all_to_all | solution.py:66
  307.9 0.2 fusion.42
  308.2 4.9 %fusion.13 = bf16[768,2048]{1,0:T(8,128)(2,1)} fusion(bf16[1024,768]{1,0:T(8,128)(2,1)S(1)} %bitcast.60, bf16[2048,2048]{1,0:T(8,128)(2,1)S(1)} %bitcast.58), kind=kOutput, calls=%fused_computation.25 | convolution fusion | flops 3222798336 | bytes 8912896 | tf_op jit(solution)/shard_map/sf,sd->fd/dot_general | solution.py:79
  313.2 0.0 reduce-scatter.5.cloned.1.call-update
  313.2 0.0 reduce-scatter.3.cloned.1.call-start
  313.2 7.1 %fusion.10 = bf16[768,2048]{1,0:T(8,128)(2,1)} fusion(bf16[1024,768]{1,0:T(8,128)(2,1)S(1)} %bitcast.59, bf16[2048,2048]{1,0:T(8,128)(2,1)} %gather_fusion), kind=kOutput, calls=%fused_computation.24 | convolution fusion | flops 3222798336 | bytes 8912896 | tf_op jit(solution)/shard_map/sf,sd->fd/dot_general | solution.py:79
  320.3 0.0 reduce-scatter.3.cloned.1.call-update
  320.3 1.4 copy-done
  321.7 0.5 fusion.22
  322.2 0.7 copy.36
  322.8 3.9 pad_maximum_fusion
  326.7 47.4 %reduce-scatter.5.cloned.1.call-done = bf16[48,2048]{1,0:T(8,128)(2,1)} async-done(((bf16[768,2048]{1,0:T(8,128)(2,1)}), bf16[48,2048]{1,0:T(8,128)(2,1)}) %reduce-scatter.5.cloned.1.call-update) | async-done | bytes 196624 | tf_op jit(solution)/shard_map/reduce_scatter | solution.py:83
  374.1 62.1 %reduce-scatter.3.cloned.1.call-done = bf16[48,2048]{1,0:T(8,128)(2,1)} async-done(((bf16[768,2048]{1,0:T(8,128)(2,1)}), bf16[48,2048]{1,0:T(8,128)(2,1)}) %reduce-scatter.3.cloned.1.call-update) | async-done | bytes 196624 | tf_op jit(solution)/shard_map/reduce_scatter | solution.py:83
  436.2 2.0 maximum_convert_fusion
  (28 shorter events, 0.1 us)
Async XLA Ops:
  7.2 174.2 %all-gather.3.cloned.1.call-start = ((), (), s32[]{:S(2)}) async-start(), calls=%async_computation.5 | async-start | bytes 6684672 | tf_op jit(solution)/shard_map/all_gather | solution.py:30
  13.2 7.6 %copy-start.2 = (s32[128,8]{0,1:T(8,128)S(1)}, s32[128,8]{0,1:T(8,128)}, u32[]{:S(2)}) copy-start(s32[128,8]{0,1:T(8,128)} %param.7) | copy-start | bytes 12292
  13.2 147.3 %all-to-all-start = ((bf16[16,128,2048]{2,1,0:T(8,128)(2,1)}), bf16[16,128,2048]{2,1,0:T(8,128)(2,1)}, u32[]{:S(2)}, u32[]{:S(2)}) async-start(bf16[16,128,2048]{2,1,0:T(8,128)(2,1)} %stack.13), calls=%async_computation | async-start | bytes 16777216 | tf_op jit(solution)/shard_map/all_to_all | solution.py:27
  197.3 5.9 %copy-start.3 = (f32[128,8]{0,1:T(8,128)S(1)}, f32[128,8]{0,1:T(8,128)}, u32[]{:S(2)}) copy-start(f32[128,8]{0,1:T(8,128)} %param.8) | copy-start | bytes 12292
  197.3 40.2 %all-to-all-start.1 = ((bf16[1,2,1024,768]{3,1,0,2:T(2,128)(2,1)}), bf16[1,2,1024,768]{3,1,0,2:T(2,128)(2,1)S(1)}, u32[]{:S(2)}, u32[]{:S(2)}) async-start(bf16[1,2,1024,768]{3,1,0,2:T(2,128)(2,1)} %copy.32), calls=%async_computation.1 | async-start | bytes 6291456 | tf_op jit(solution)/shard_map/all_to_all | solution.py:70
  202.8 171.3 %reduce-scatter.5.cloned.1.call-start = ((), (), s32[]{:S(2)}) async-start(), calls=%async_computation.7 | async-start | bytes 3342336 | tf_op jit(solution)/shard_map/reduce_scatter | solution.py:83
  237.5 1.7 copy-start.1
  261.3 46.9 %slice-start = ((s8[8388608]{0:T(1024)(128)(4,1)}), s8[4194304]{0:T(1024)(128)(4,1)S(1)}, s32[]{:S(2)}) async-start(s8[8388608]{0:T(1024)(128)(4,1)} %bitcast.57), calls=%async_computation.8 | async-start | bytes 8388608
  263.5 44.7 %slice-start.1 = ((s8[8388608]{0:T(1024)(128)(4,1)}), s8[4194304]{0:T(1024)(128)(4,1)S(1)}, s32[]{:S(2)}) async-start(s8[8388608]{0:T(1024)(128)(4,1)} %bitcast.57), calls=%async_computation.9 | async-start | bytes 8388608
  313.2 123.0 %reduce-scatter.3.cloned.1.call-start = ((), (), s32[]{:S(2)}) async-start(), calls=%async_computation.6 | async-start | bytes 3342336 | tf_op jit(solution)/shard_map/reduce_scatter | solution.py:83
  320.3 1.4 copy-start
Sparse Core Ops, SparseCore 0:
  9.8 48.9 all-gather.2
  313.3 60.7 reduce-scatter.4
  376.7 59.4 reduce-scatter.2
